TPU v7x, 32 devices: a whole 2x2x4 slice. The times are simulated.
32 devices in a mesh: seq: 2 (over y), fsdp: 16 (over z, x, core).
Axes of the slice: x: 2, y: 2, z: 4, core: 2. Of those that a mesh axis runs over, the one named last changes fastest.
Arguments:
- tokens: bfloat16 [16, 1024, 1024], P('fsdp', 'seq'), may hold values from -6 to 6
- blocks: int32 [16, 1024], P('fsdp'), may hold values from 0 to 7, never falling along the last dimension, each value on 1 to 256 neighbouring positions
- first_gain: bfloat16 [1024], P('fsdp'), may hold values from 0.5 to 1.5
- first_shift: bfloat16 [1024], P('fsdp'), may hold values from -1.5 to 1.5
- joint_weight: bfloat16 [1024, 3072], P('fsdp'), may hold values from -0.1875 to 0.1875
- joint_bias: bfloat16 [2, 1024], P(None, 'fsdp'), may hold values from -1.5 to 1.5
- output_weight: bfloat16 [1024, 1024], P('fsdp'), may hold values from -0.75 to 0.75
- output_bias: bfloat16 [1024], P('fsdp'), may hold values from -1.5 to 1.5
- second_gain: bfloat16 [1024], P('fsdp'), may hold values from 0.5 to 1.5
- second_shift: bfloat16 [1024], P('fsdp'), may hold values from -1.5 to 1.5
- upward_weight: bfloat16 [1024, 4096], P('fsdp'), may hold values from -0.1875 to 0.1875
- upward_bias: bfloat16 [4096], P('fsdp'), may hold values from -1.5 to 1.5
- downward_weight: bfloat16 [4096, 1024], P('fsdp'), may hold values from -0.125 to 0.125
- downward_bias: bfloat16 [1024], P('fsdp'), may hold values from -1.5 to 1.5
- cotangent: bfloat16 [16, 1024, 1024], P('fsdp', 'seq'), may hold values from -6 to 6
Outputs:
- result: bfloat16 [16, 1024, 1024], P('fsdp', 'seq')
- grad_tokens: float32 [16, 1024, 1024], P('fsdp', 'seq')
- grad_first_gain: float32 [1024], P('fsdp')
- grad_first_shift: float32 [1024], P('fsdp')
- grad_joint_weight: float32 [1024, 3072], P('fsdp')
- grad_joint_bias: float32 [2, 1024], P(None, 'fsdp')
- grad_output_weight: float32 [1024, 1024], P('fsdp')
- grad_output_bias: float32 [1024], P('fsdp')
- grad_second_gain: float32 [1024], P('fsdp')
- grad_second_shift: float32 [1024], P('fsdp')
- grad_upward_weight: float32 [1024, 4096], P('fsdp')
- grad_upward_bias: float32 [4096], P('fsdp')
- grad_downward_weight: float32 [4096, 1024], P('fsdp')
- grad_downward_bias: float32 [1024], P('fsdp')
Inputs may be any that keep to these rules, and one draw needn't show every extreme that they name: `blocks`: along each sequence the block number never falls; every block has 1 to 256 tokens, and one has exactly 256.
All inputs are finite; a program needn't handle non-finite values.
Results may differ from a plain program's by a relative error of at most 0.014.
Values may be sent and summed in bfloat16 or wider, within the bound.
No kernel may reach another device: no remote copies, remote signals or barrier semaphores. Data moves between devices by JAX's collectives and lax.ppermute only.
A program may use at most 192 MiB of HBM per device.

v0:
```python
import jax
import jax.numpy as jnp
from jax import lax
from jax.sharding import PartitionSpec as P

HEADS = 16
HEAD_DIM = 64
EPSILON = 1e-05


def scaled_norm(values, gain):
    center = values - jnp.mean(values, axis=-1, keepdims=True)
    spread = jnp.mean(center * center, axis=-1, keepdims=True)
    return center * lax.rsqrt(spread + EPSILON) * gain


def gelu_tanh(values):
    return jax.nn.gelu(values, approximate=True)


def matmul(left, right):
    return jnp.dot(left, right, preferred_element_type=jnp.float32)


def left_contract(left, right):
    return lax.dot_general(
        left, right, (((0,), (0,)), ((), ())), preferred_element_type=jnp.float32
    )


def right_contract(left, right):
    return lax.dot_general(
        left, right, (((1,), (1,)), ((), ())), preferred_element_type=jnp.float32
    )


def masked_scores(queries, keys_in, slope, distance, allowed):
    scores = right_contract(queries, keys_in) * HEAD_DIM ** (-0.5) - slope * distance
    return jnp.where(allowed, scores, -1e30)


def attend_heads(heads, slopes, distance, allowed):

    def one_head(packed):
        queries, keys_in, values_in, slope = packed
        scores = masked_scores(queries, keys_in, slope, distance, allowed)
        top_score = jnp.max(scores, axis=1, keepdims=True)
        totals = jnp.sum(jnp.exp(scores - top_score), axis=1, keepdims=True)
        log_total = top_score + jnp.log(totals)
        probs = jnp.exp(scores - log_total).astype(jnp.bfloat16)
        return (matmul(probs, values_in).astype(jnp.bfloat16), log_total[:, 0])

    return lax.map(one_head, (heads[0], heads[1], heads[2], slopes))


def attend_back(heads, log_totals, grad_heads, slopes, distance, allowed):

    def one_head(packed):
        queries, keys_in, values_in, log_total, grad_head, slope = packed
        scores = masked_scores(queries, keys_in, slope, distance, allowed)
        probs = jnp.exp(scores - log_total[:, None])
        grad_probs = right_contract(grad_head, values_in)
        inner = jnp.sum(probs * grad_probs, axis=1, keepdims=True)
        grad_scores = (probs * (grad_probs - inner)).astype(jnp.bfloat16)
        factor = HEAD_DIM ** (-0.5)
        grad_queries = matmul(grad_scores, keys_in) * factor
        grad_keys = left_contract(grad_scores, queries) * factor
        grad_values = left_contract(probs.astype(jnp.bfloat16), grad_head)
        return jnp.stack([grad_queries, grad_keys, grad_values]).astype(jnp.bfloat16)

    return lax.map(one_head, (heads[0], heads[1], heads[2], log_totals, grad_heads, slopes))


def per_device(
    tokens,
    blocks,
    first_gain,
    first_shift,
    joint_weight,
    joint_bias,
    output_weight,
    output_bias,
    second_gain,
    second_shift,
    upward_weight,
    upward_bias,
    downward_weight,
    downward_bias,
    cotangent,
):
    groups = lax.axis_size("seq")
    token_count = tokens.shape[1]
    model_width = tokens.shape[2]
    seq_length = token_count * groups
    local_heads = HEADS // groups
    group_width = model_width // groups
    inputs = tokens[0].astype(jnp.float32)
    attn_set = (
        lax.all_gather(first_gain, "fsdp", axis=0, tiled=True),
        lax.all_gather(first_shift, "fsdp", axis=0, tiled=True),
        lax.all_gather(joint_weight, "fsdp", axis=0, tiled=True),
        lax.all_gather(joint_bias, "fsdp", axis=1, tiled=True),
        lax.all_gather(output_weight, "fsdp", axis=0, tiled=True),
        lax.all_gather(output_bias, "fsdp", axis=0, tiled=True),
    )
    normed_one = (
        scaled_norm(inputs, attn_set[0].astype(jnp.float32)) + attn_set[1].astype(jnp.float32)
    ).astype(jnp.bfloat16)
    bias_full = jnp.concatenate(
        [attn_set[3][0], jnp.zeros((model_width,), jnp.bfloat16), attn_set[3][1]]
    ).astype(jnp.float32)
    joint = (matmul(normed_one, attn_set[2]) + bias_full).astype(jnp.bfloat16)
    joint = joint.reshape(token_count, 3, groups, group_width)
    heads = lax.all_to_all(joint, "seq", split_axis=2, concat_axis=0, tiled=True)
    heads = heads.reshape(seq_length, 3, local_heads, HEAD_DIM).transpose(1, 2, 0, 3)
    positions = jnp.arange(seq_length)
    distance = jnp.abs(positions[:, None] - positions[None, :]).astype(jnp.float32)
    block_row = blocks[0]
    allowed = block_row[None, :] <= block_row[:, None]
    head_index = lax.axis_index("seq") * local_heads + jnp.arange(local_heads)
    slopes = jnp.exp2(-8.0 * (head_index.astype(jnp.float32) + 1.0) / HEADS)
    attended, log_totals = attend_heads(heads, slopes, distance, allowed)
    flat_heads = attended.transpose(1, 0, 2).reshape(seq_length, 1, group_width)
    mixed = lax.all_to_all(flat_heads, "seq", split_axis=0, concat_axis=1, tiled=True).reshape(
        token_count, model_width
    )
    hidden = inputs + matmul(mixed, attn_set[4]) + attn_set[5].astype(jnp.float32)
    mlp_set = (
        lax.all_gather(second_gain, "fsdp", axis=0, tiled=True),
        lax.all_gather(second_shift, "fsdp", axis=0, tiled=True),
        lax.all_gather(upward_weight, "fsdp", axis=0, tiled=True),
        lax.all_gather(upward_bias, "fsdp", axis=0, tiled=True),
        lax.all_gather(downward_weight, "fsdp", axis=0, tiled=True),
        lax.all_gather(downward_bias, "fsdp", axis=0, tiled=True),
    )
    normed_two = (
        scaled_norm(hidden, mlp_set[0].astype(jnp.float32)) + mlp_set[1].astype(jnp.float32)
    ).astype(jnp.bfloat16)
    upward = matmul(normed_two, mlp_set[2]) + mlp_set[3].astype(jnp.float32)
    activated = gelu_tanh(upward).astype(jnp.bfloat16)
    output = hidden + matmul(activated, mlp_set[4]) + mlp_set[5].astype(jnp.float32)
    back_gain_two, back_upward, back_downward = (
        lax.all_gather(second_gain, "fsdp", axis=0, tiled=True),
        lax.all_gather(upward_weight, "fsdp", axis=0, tiled=True),
        lax.all_gather(downward_weight, "fsdp", axis=0, tiled=True),
    )
    grad_output = cotangent[0].astype(jnp.float32)
    grad_low = grad_output.astype(jnp.bfloat16)
    grad_down_bias = jnp.sum(grad_low.astype(jnp.float32), axis=0)
    grad_down_weight = left_contract(activated, grad_low)
    grad_act = right_contract(grad_low, back_downward)
    gelu_back = jax.vjp(gelu_tanh, upward)[1]
    grad_up = gelu_back(grad_act)[0].astype(jnp.bfloat16)
    grad_up_bias = jnp.sum(grad_up.astype(jnp.float32), axis=0)
    grad_up_weight = left_contract(normed_two, grad_up)
    grad_normed_two = right_contract(grad_up, back_upward)
    norm_two_back = jax.vjp(scaled_norm, hidden, back_gain_two.astype(jnp.float32))[1]
    grad_hidden_norm, grad_gain_two = norm_two_back(grad_normed_two)
    grad_shift_two = jnp.sum(grad_normed_two, axis=0)
    grad_hidden = grad_output + grad_hidden_norm
    back_gain_one, back_joint, back_output = (
        lax.all_gather(first_gain, "fsdp", axis=0, tiled=True),
        lax.all_gather(joint_weight, "fsdp", axis=0, tiled=True),
        lax.all_gather(output_weight, "fsdp", axis=0, tiled=True),
    )
    hidden_low = grad_hidden.astype(jnp.bfloat16)
    grad_out_bias = jnp.sum(hidden_low.astype(jnp.float32), axis=0)
    grad_out_weight = left_contract(mixed, hidden_low)
    grad_mixed = right_contract(hidden_low, back_output).astype(jnp.bfloat16)
    grad_mixed = grad_mixed.reshape(token_count, groups, group_width)
    grad_heads = lax.all_to_all(grad_mixed, "seq", split_axis=1, concat_axis=0, tiled=True)
    grad_heads = grad_heads.reshape(seq_length, local_heads, HEAD_DIM).transpose(1, 0, 2)
    grad_stack = attend_back(heads, log_totals, grad_heads, slopes, distance, allowed)
    grad_stack = grad_stack.transpose(2, 1, 0, 3).reshape(seq_length, 3, 1, group_width)
    grad_joint = lax.all_to_all(grad_stack, "seq", split_axis=0, concat_axis=2, tiled=True)
    grad_joint = grad_joint.reshape(token_count, 3 * model_width)
    joint_sums = jnp.sum(grad_joint.astype(jnp.float32), axis=0)
    grad_joint_bias = jnp.stack([joint_sums[:model_width], joint_sums[2 * model_width :]])
    grad_joint_weight = left_contract(normed_one, grad_joint)
    grad_normed_one = right_contract(grad_joint, back_joint)
    norm_one_back = jax.vjp(scaled_norm, inputs, back_gain_one.astype(jnp.float32))[1]
    grad_input_norm, grad_gain_one = norm_one_back(grad_normed_one)
    grad_shift_one = jnp.sum(grad_normed_one, axis=0)
    grad_inputs = grad_hidden + grad_input_norm
    every_sum = (
        lax.psum_scatter(grad_gain_one, "fsdp", scatter_dimension=0, tiled=True),
        lax.psum_scatter(grad_shift_one, "fsdp", scatter_dimension=0, tiled=True),
        lax.psum_scatter(grad_joint_weight, "fsdp", scatter_dimension=0, tiled=True),
        lax.psum_scatter(grad_joint_bias, "fsdp", scatter_dimension=1, tiled=True),
        lax.psum_scatter(grad_out_weight, "fsdp", scatter_dimension=0, tiled=True),
        lax.psum_scatter(grad_out_bias, "fsdp", scatter_dimension=0, tiled=True),
        lax.psum_scatter(grad_gain_two, "fsdp", scatter_dimension=0, tiled=True),
        lax.psum_scatter(grad_shift_two, "fsdp", scatter_dimension=0, tiled=True),
        lax.psum_scatter(grad_up_weight, "fsdp", scatter_dimension=0, tiled=True),
        lax.psum_scatter(grad_up_bias, "fsdp", scatter_dimension=0, tiled=True),
        lax.psum_scatter(grad_down_weight, "fsdp", scatter_dimension=0, tiled=True),
        lax.psum_scatter(grad_down_bias, "fsdp", scatter_dimension=0, tiled=True),
    )
    attn_sums = every_sum[:6]
    mlp_sums = every_sum[6:]
    totals = (
        lax.psum(attn_sums[0].astype(jnp.bfloat16), "seq").astype(jnp.float32),
        lax.psum(attn_sums[1].astype(jnp.bfloat16), "seq").astype(jnp.float32),
        lax.psum(attn_sums[2].astype(jnp.bfloat16), "seq").astype(jnp.float32),
        lax.psum(attn_sums[3].astype(jnp.bfloat16), "seq").astype(jnp.float32),
        lax.psum(attn_sums[4].astype(jnp.bfloat16), "seq").astype(jnp.float32),
        lax.psum(attn_sums[5].astype(jnp.bfloat16), "seq").astype(jnp.float32),
        lax.psum(mlp_sums[0].astype(jnp.bfloat16), "seq").astype(jnp.float32),
        lax.psum(mlp_sums[1].astype(jnp.bfloat16), "seq").astype(jnp.float32),
        lax.psum(mlp_sums[2].astype(jnp.bfloat16), "seq").astype(jnp.float32),
        lax.psum(mlp_sums[3].astype(jnp.bfloat16), "seq").astype(jnp.float32),
        lax.psum(mlp_sums[4].astype(jnp.bfloat16), "seq").astype(jnp.float32),
        lax.psum(mlp_sums[5].astype(jnp.bfloat16), "seq").astype(jnp.float32),
    )
    return (
        output.astype(jnp.bfloat16)[None],
        grad_inputs[None],
        totals[0],
        totals[1],
        totals[2],
        totals[3],
        totals[4],
        totals[5],
        totals[6],
        totals[7],
        totals[8],
        totals[9],
        totals[10],
        totals[11],
    )


def solution(mesh):
    in_specs = (
        P("fsdp", "seq", None),
        P("fsdp", None),
        P("fsdp"),
        P("fsdp"),
        P("fsdp", None),
        P(None, "fsdp"),
        P("fsdp", None),
        P("fsdp"),
        P("fsdp"),
        P("fsdp"),
        P("fsdp", None),
        P("fsdp"),
        P("fsdp", None),
        P("fsdp"),
        P("fsdp", "seq", None),
    )
    out_specs = (
        P("fsdp", "seq", None),
        P("fsdp", "seq", None),
        P("fsdp"),
        P("fsdp"),
        P("fsdp", None),
        P(None, "fsdp"),
        P("fsdp", None),
        P("fsdp"),
        P("fsdp"),
        P("fsdp"),
        P("fsdp", None),
        P("fsdp"),
        P("fsdp", None),
        P("fsdp"),
    )
    return jax.shard_map(
        per_device, mesh=mesh, in_specs=in_specs, out_specs=out_specs, check_vma=False
    )
```

profile of v0, /device:TPU:0, one launch (start us, length us, event | category | flops | bytes accessed | tf_op | source)
XLA Modules:
  0.0 1121.6 jit_solution(8430259839319301549)
XLA Ops:
  10.1 23.6 %all-gather = bf16[16,64,2]{1,2,0:T(2,128)(2,1)S(1)} all-gather(bf16[1,64,2]{1,2,0:T(2,128)(2,1)} %bitcast.245), channel_id=1, replica_groups=mesh['seq'=2,'fsdp'=16] {'fsdp'}, dimensions={0}, use_global_device_ids=true | all-gather | bytes 4352 | tf_op jit(solution)/shard_map/all_gather | solution.py:102
  38.8 59.6 %all-reduce.14 = (bf16[1024]{0:T(1024)(128)(2,1)S(1)}, bf16[1024]{0:T(1024)(128)(2,1)S(1)}, bf16[1024]{0:T(1024)(128)(2,1)S(1)}, bf16[1024]{0:T(1024)(128)(2,1)}...) all-reduce(bf16[1024]{0:T(1024)(128)(2,1)S(1)} %dynamic-update-slic, ...), channel_id=1, replica_groups=mesh['seq'=2,'fsdp'=16] {'fsdp'}, use_global_device_ids=true, to_apply=%add.1 | all-reduce | flops 6144 | bytes 24576
  98.5 8.1 add_convert_fusion
  106.7 8.3 reshape.247
  115.0 8.6 copy.73
  123.6 5.5 all-to-all-start
  129.2 31.7 %all-to-all-done = bf16[512,3,2,512]{0,3,1,2:T(8,128)(2,1)} async-done(((bf16[512,3,2,512]{0,3,1,2:T(8,128)(2,1)}), bf16[512,3,2,512]{0,3,1,2:T(8,128)(2,1)}, u32[]{:S(2)}, u32[]{:S(2)}) %all-to-all-start) | async-done | bytes 3145760 | tf_op jit(solution)/shard_map/all_to_all | solution.py:114
  160.9 6.8 copy.74
  167.7 6.1 reshape.248
  182.7 47.9 %while.24 = (s32[]{:T(128)}, bf16[8,1024,64]{1,2,0:T(8,128)(2,1)}, f32[8,1024]{1,0:T(8,128)S(1)}, bf16[8,1024,64]{2,1,0:T(8,128)(2,1)}, bf16[8,1024,64]{2,1,0:T(...) while((s32[]{:T(128)}, bf16[8,1024,64]{1,2,0:T(8,128)(2,1)}, ...), condition=%wide.region_5.6_spmd.clone, body=%wide.region_2.5_spmd.clone.sunk | while | flops 282131456 | bytes 13548157 | solution.py:53
  239.5 4.4 all-to-all-start.1
  244.0 19.0 %all-gather.1 = bf16[16,1,256]{2,1,0:T(2,128)(2,1)S(1)} all-gather(bf16[1,1,256]{2,1,0:T(2,128)(2,1)S(1)} %reshape.275), channel_id=1, replica_groups=mesh['seq'=2,'fsdp'=16] {'fsdp'}, dimensions={0}, use_global_device_ids=true | all-gather | bytes 8704 | tf_op jit(solution)/shard_map/all_gather | solution.py:132
  272.3 10.6 fusion.109
  282.9 14.3 %convert_reduce_fusion = (f32[4096]{0:T(1024)}, bf16[512,4096]{1,0:T(8,128)(2,1)S(1)}) fusion(f32[512,4096]{1,0:T(8,128)} %fusion.109, f32[4096]{0:T(1024)S(1)} %bitcast.240, bf16[4096,1024]{1,0:T(8,128)(2,1)} %all-gather.13.cloned.1.call-done, bf16[1,512,1024]{2,1,0:T(8,128)(2,1)S(1)} %copy-done.6), kind=kOutput, calls=%fused_computation.72 | convolution fusion | flops 4343197696 | bytes 22052864 | tf_op jit(solution)/shard_map/dot_general | solution.py:32
  297.2 5.0 multiply_reduce_fusion.1
  315.0 10.9 all-to-all-done.2
  327.9 99.5 %while.25 = (s32[]{:T(128)}, bf16[8,3,1024,64]{2,3,0,1:T(8,128)(2,1)}, bf16[8,1024,64]{2,1,0:T(8,128)(2,1)}, bf16[8,1024,64]{2,1,0:T(8,128)(2,1)}, f32[8]{0:T(12...) while((s32[]{:T(128)}, ...), condition=%wide.region_12.13_spmd.clone, body=%wide.region_10.12_spmd.clone.sunk | while | flops 688323584 | bytes 34241164 | solution.py:71
  330.1 4.3 multiply_reduce_fusion.5
  342.6 4.3 multiply_reduce_fusion.5
  427.3 7.6 copy.87
  434.9 51.4 %all_to_all.60 = bf16[1024,3,1,512]{3,1,2,0:T(4,128)(2,1)S(1)} all-to-all(bf16[1024,3,1,512]{3,1,2,0:T(4,128)(2,1)} %copy.87), channel_id=1, replica_groups=mesh['seq'=2,'fsdp'=16] {'seq'}, dimensions={0} | all-to-all | bytes 6291456 | tf_op jit(solution)/shard_map/all_to_all | solution.py:175
  490.0 10.5 fusion.88
  500.8 16.2 %fusion.108 = f32[1024,4096]{1,0:T(8,128)} fusion(bf16[512,4096]{1,0:T(8,128)(2,1)} %copy-done.33, f32[512,1024]{1,0:T(8,128)} %copy-done.4, f32[1024]{0:T(1024)S(1)} %convert_element_type.192, f32[1024]{0:T(1024)S(1)} %convert_element_type.191, f32[512]{0:T(512)S(1)} %fusion.106, f32[512]{0:T(512)S(1)} %broadcast_multiply_fusion), kind=kOutput, calls=%fused_computation.153 | convolution fusion | flops 4297588736 | bytes 23080960 | tf_op jit(solution)/shard_map/dot_general | solution.py:26
  517.1 17.9 %fusion.91 = f32[4096,1024]{1,0:T(8,128)} fusion(bf16[1,512,1024]{2,1,0:T(8,128)(2,1)} %param.33, f32[512,4096]{1,0:T(8,128)} %fusion.109, f32[4096]{0:T(1024)S(1)} %bitcast.241), kind=kOutput, calls=%fused_computation.116 | convolution fusion | flops 4315938816 | bytes 26230784 | tf_op jit(solution)/shard_map/dot_general | solution.py:26
  538.8 12.9 %fusion.85 = bf16[1,512,1024]{2,1,0:T(8,128)(2,1)} fusion(f32[512,1024]{1,0:T(8,128)} %copy-done.4, bf16[4096,1024]{1,0:T(8,128)(2,1)} %all-gather.13.cloned.1.call-done, f32[1024]{0:T(1024)S(1)} %convert_element_type.196, f32[512,4096]{1,0:T(8,128)} %fusion.109, f32[4096]{0:T(1024)S(1)} %bitcast.242), kind=kOutput, calls=%fused_computation.109 | convolution fusion | flops 4317511680 | bytes 19943424 | tf_op jit(solution)/shard_map/dot_general | solution.py:22
  553.4 79.2 %reduce-scatter.8.cloned.1.call-done = f32[64,3072]{1,0:T(8,128)} async-done(((f32[1024,3072]{1,0:T(8,128)}), f32[64,3072]{1,0:T(8,128)}) %reduce-scatter.8.cloned.1.call-update) | async-done | bytes 786448 | tf_op jit(solution)/shard_map/reduce_scatter | solution.py:188
  634.5 178.8 %reduce-scatter.12.cloned.1.call-done = f32[64,4096]{1,0:T(8,128)} async-done(((f32[1024,4096]{1,0:T(8,128)}), f32[64,4096]{1,0:T(8,128)}) %reduce-scatter.12.cloned.1.call-update) | async-done | bytes 1048592 | tf_op jit(solution)/shard_map/reduce_scatter | solution.py:194
  815.4 178.5 %reduce-scatter.14.cloned.1.call-done = f32[256,1024]{1,0:T(8,128)} async-done(((f32[4096,1024]{1,0:T(8,128)}), f32[256,1024]{1,0:T(8,128)}) %reduce-scatter.14.cloned.1.call-update) | async-done | bytes 1048592 | tf_op jit(solution)/shard_map/reduce_scatter | solution.py:196
  996.1 6.9 fusion.110
  1007.0 59.6 %all-reduce.13 = (bf16[1024]{0:T(1024)(128)(2,1)S(1)}, bf16[1024]{0:T(1024)(128)(2,1)S(1)}, bf16[1024]{0:T(1024)(128)(2,1)S(1)}, bf16[1024]{0:T(1024)(128)(2,1)S...) all-reduce(f32[1024]{0:T(1024)S(1)} %get-tuple-element.229, ...), channel_id=2, replica_groups=mesh['seq'=2,'fsdp'=16] {'fsdp'}, use_global_device_ids=true, to_apply=%region_16.17.clone | all-reduce | flops 10240 | bytes 61440
  1068.0 5.1 all-reduce.15
  1077.3 30.3 %all-reduce.19.cloned.1.call-done = (bf16[64,3072]{1,0:T(8,128)(2,1)}, bf16[64,1024]{1,0:T(8,128)(2,1)}, bf16[64,4096]{1,0:T(8,128)(2,1)}, bf16[256,1024]{1,0:T(8,128)(2,1)}) async-done(((bf16[64,3072]{1,0:T(8,128)(2,1)}, bf16[64,1024]{1,0:T(8,128)(2,1)}, bf16[64,4096]{1,0:T(8,128)(2,1)}, bf16[256,1024]{1,0:T(8,128)(2,1)}), (bf16[64,3072]{1,0:T(8,128)(2,1)}, bf16[64,1024]{1,0:T(8,128)(2,1)}, ...) | async-done | bytes 1572880 | tf_op jit(solution)/shard_map/psum | solution.py:204
  (308 shorter events, 217.9 us)
Async XLA Ops:
  7.2 29.0 %copy-start.23 = (u32[32]{0:T(128)S(1)}, u32[32]{0:T(128)}, u32[]{:S(2)}) copy-start(u32[32]{0:T(128)} %constant.97) | copy-start | bytes 388
  7.2 28.0 %copy-start = (bf16[1,512,1024]{2,1,0:T(8,128)(2,1)S(1)}, bf16[1,512,1024]{2,1,0:T(8,128)(2,1)}, u32[]{:S(2)}) copy-start(bf16[1,512,1024]{2,1,0:T(8,128)(2,1)} %param.19) | copy-start | bytes 3145732
  7.2 30.2 %copy-start.26 = (bf16[64]{0:T(256)(128)(2,1)S(1)}, bf16[64]{0:T(256)(128)(2,1)}, u32[]{:S(2)}) copy-start(bf16[64]{0:T(256)(128)(2,1)} %param.22) | copy-start | bytes 388
  7.2 30.5 %copy-start.27 = (bf16[64]{0:T(256)(128)(2,1)S(1)}, bf16[64]{0:T(256)(128)(2,1)}, u32[]{:S(2)}) copy-start(bf16[64]{0:T(256)(128)(2,1)} %param.21) | copy-start | bytes 388
  7.2 30.7 %copy-start.28 = (bf16[64]{0:T(256)(128)(2,1)S(1)}, bf16[64]{0:T(256)(128)(2,1)}, u32[]{:S(2)}) copy-start(bf16[64]{0:T(256)(128)(2,1)} %param.26) | copy-start | bytes 388
  7.2 30.9 %copy-start.29 = (bf16[64]{0:T(256)(128)(2,1)S(1)}, bf16[64]{0:T(256)(128)(2,1)}, u32[]{:S(2)}) copy-start(bf16[64]{0:T(256)(128)(2,1)} %param.32) | copy-start | bytes 388
  7.2 31.1 %copy-start.30 = (bf16[64]{0:T(256)(128)(2,1)S(1)}, bf16[64]{0:T(256)(128)(2,1)}, u32[]{:S(2)}) copy-start(bf16[64]{0:T(256)(128)(2,1)} %param.28) | copy-start | bytes 388
  7.3 31.4 %copy-start.31 = (bf16[64]{0:T(256)(128)(2,1)S(1)}, bf16[64]{0:T(256)(128)(2,1)}, u32[]{:S(2)}) copy-start(bf16[64]{0:T(256)(128)(2,1)} %param.27) | copy-start | bytes 388
  7.3 91.3 %all-gather.7.cloned.1.call-start = ((), (), s32[]{:S(2)}) async-start(), calls=%async_computation.9 | async-start | bytes 6684672 | tf_op jit(solution)/shard_map/all_gather | solution.py:101
  8.0 260.6 %all-gather.9.cloned.1.call-start = ((), (), s32[]{:S(2)}) async-start(), calls=%async_computation.10 | async-start | bytes 2228224 | tf_op jit(solution)/shard_map/all_gather | solution.py:103
  8.7 263.5 %all-gather.11.cloned.1.call-start = ((), (), s32[]{:S(2)}) async-start(), calls=%async_computation.11 | async-start | bytes 8912896 | tf_op jit(solution)/shard_map/all_gather | solution.py:131
  9.5 273.4 %all-gather.13.cloned.1.call-start = ((), (), s32[]{:S(2)}) async-start(), calls=%async_computation.12 | async-start | bytes 8912896 | tf_op jit(solution)/shard_map/all_gather | solution.py:133
  35.2 71.5 %copy-start.13 = (f32[512]{0:T(512)}, f32[512]{0:T(512)S(1)}, u32[]{:S(2)}) copy-start(f32[512]{0:T(512)S(1)} %broadcast_multiply_fusion.1) | copy-start | bytes 6148
  35.6 71.1 %copy-start.15 = (f32[512]{0:T(512)}, f32[512]{0:T(512)S(1)}, u32[]{:S(2)}) copy-start(f32[512]{0:T(512)S(1)} %fusion.105) | copy-start | bytes 6148
  98.5 8.2 copy-start.20
  98.5 8.2 copy-start.11
  123.6 37.3 %all-to-all-start = ((bf16[512,3,2,512]{0,3,1,2:T(8,128)(2,1)}), bf16[512,3,2,512]{0,3,1,2:T(8,128)(2,1)}, u32[]{:S(2)}, u32[]{:S(2)}) async-start(bf16[512,3,2,512]{0,3,1,2:T(8,128)(2,1)} %copy.73), calls=%async_computation | async-start | bytes 6291456 | tf_op jit(solution)/shard_map/all_to_all | solution.py:114
  230.6 8.9 copy-start.5
  234.6 9.4 copy-start.32
  239.5 23.5 %all-to-all-start.1 = ((bf16[2,2,131072]{2,1,0:T(2,128)(2,1)}), bf16[2,2,131072]{2,1,0:T(2,128)(2,1)}, u32[]{:S(2)}, u32[]{:S(2)}) async-start(bf16[2,2,131072]{2,1,0:T(2,128)(2,1)} %reshape.301), calls=%async_computation.1 | async-start | bytes 2097152 | tf_op jit(solution)/shard_map/all_to_all | solution.py:124
  271.8 30.4 %copy-start.4 = (f32[512,1024]{1,0:T(8,128)}, f32[512,1024]{1,0:T(8,128)S(1)}, u32[]{:S(2)}) copy-start(f32[512,1024]{1,0:T(8,128)S(1)} %get-tuple-element.313) | copy-start | bytes 6291460
  272.2 10.7 copy-start.6
  282.9 14.3 %copy-start.24 = (bf16[1024,4096]{1,0:T(8,128)(2,1)S(1)}, bf16[1024,4096]{1,0:T(8,128)(2,1)}, u32[]{:S(2)}) copy-start(bf16[1024,4096]{1,0:T(8,128)(2,1)} %all-gather.11.cloned.1.call-done) | copy-start | bytes 25165828
  307.9 17.9 %all-to-all-start.2 = ((bf16[512,2,512]{0,2,1:T(8,128)(2,1)}), bf16[512,2,512]{0,2,1:T(8,128)(2,1)S(1)}, u32[]{:S(2)}, u32[]{:S(2)}) async-start(bf16[512,2,512]{0,2,1:T(8,128)(2,1)} %bitcast.19), calls=%async_computation.2 | async-start | bytes 2097152 | tf_op jit(solution)/shard_map/all_to_all | solution.py:171
  311.5 240.2 %reduce-scatter.10.cloned.1.call-start = ((), (), s32[]{:S(2)}) async-start(), calls=%async_computation.14 | async-start | bytes 4456448 | tf_op jit(solution)/shard_map/reduce_scatter | solution.py:190
  314.9 317.7 %reduce-scatter.8.cloned.1.call-start = ((), (), s32[]{:S(2)}) async-start(), calls=%async_computation.13 | async-start | bytes 13369344 | tf_op jit(solution)/shard_map/reduce_scatter | solution.py:188
  500.5 312.8 %reduce-scatter.12.cloned.1.call-start = ((), (), s32[]{:S(2)}) async-start(), calls=%async_computation.15 | async-start | bytes 17825792 | tf_op jit(solution)/shard_map/reduce_scatter | solution.py:194
  517.0 476.9 %reduce-scatter.14.cloned.1.call-start = ((), (), s32[]{:S(2)}) async-start(), calls=%async_computation.16 | async-start | bytes 17825792 | tf_op jit(solution)/shard_map/reduce_scatter | solution.py:196
  535.0 532.1 %reduce-scatter.16.cloned.1.call-start = ((), (), s32[]{:S(2)}) async-start(), calls=%async_computation.17 | async-start | bytes 557056
  538.5 569.1 %all-reduce.19.cloned.1.call-start = ((), (), s32[]{:S(2)}) async-start(), calls=%async_computation.18 | async-start | bytes 3145728 | tf_op jit(solution)/shard_map/psum | solution.py:204
  551.7 444.4 %copy-start.1 = (bf16[1,512,1024]{2,1,0:T(8,128)(2,1)S(1)}, bf16[1,512,1024]{2,1,0:T(8,128)(2,1)}, u32[]{:S(2)}) copy-start(bf16[1,512,1024]{2,1,0:T(8,128)(2,1)} %param.19) | copy-start | bytes 3145732
  996.1 6.9 copy-start.18
  (15 other events, 41.5 us)
Sparse Core Ops, SparseCore 0:
  10.4 64.7 all-gather.6
  77.3 40.1 all-gather.8
  119.6 72.9 all-gather.10
  194.7 72.9 all-gather.12
  315.8 70.6 reduce-scatter.9
  500.7 131.9 reduce-scatter.7
  636.7 176.6 reduce-scatter.11
  817.5 176.4 reduce-scatter.13
  998.1 55.2 reduce-scatter.15
  1056.8 50.7 all-reduce.18
where the time goes:
time: 1130 us; the launch traced here: 1120 us
  waiting for transfers between devices  512 us (45%)
  matrix products  227 us (20%)
  blocking collectives  218 us (19%)
  local copies, waits for them, and re-layouts  82.9 us (7%)
  other arithmetic  49.6 us (4%)
  between operations  17.2 us (2%)
  starting transfers between devices  14.4 us (1%)
    reduce_scatter x1, waiting for transfers between devices, per_device(): lax.psum_scatter(grad_up_weight, 'fsdp', scatter_dimension=0, tiled=True)  179 us
    reduce_scatter x1, waiting for transfers between devices, per_device(): lax.psum_scatter(grad_down_weight, 'fsdp', scatter_dimension=0, tiled=True)  178 us
    unnamed x2, blocking collectives  119 us
    dot_general x28, matrix products, right_contract(): lax.dot_general(left, right, (((1,), (1,)), ((), ())), preferred_element_...  100 us
    reduce_scatter x1, waiting for transfers between devices, per_device(): lax.psum_scatter(grad_joint_weight, 'fsdp', scatter_dimension=0, tiled=True)  79.2 us
    dot_general x20, matrix products, left_contract(): lax.dot_general(left, right, (((0,), (0,)), ((), ())), preferred_element_...  67.8 us
    dot_general x20, matrix products, matmul(): return jnp.dot(left, right, preferred_element_type=jnp.float32)  58.5 us
    all_to_all x1, blocking collectives, per_device(): lax.all_to_all(grad_stack, 'seq', split_axis=0, concat_axis=2, tiled=True)  51.4 us
  transfers between devices with their start and end apart: 13, of which 6 were waited for; matrix products, arithmetic and copies ran while one was open for 29% of the time, Pallas kernels for 0%

commit v1 on v0

--- a/solution.py
+++ b/solution.py
@@ -6,6 +6,19 @@
 HEADS = 16
 HEAD_DIM = 64
 EPSILON = 1e-05
+
+
+def collect(x, axis, dim):
+    ways = lax.axis_size(axis)
+    up = [(d, (d + 1) % ways) for d in range(ways)]
+    down = [(d, (d - 1) % ways) for d in range(ways)]
+    earlier, later = ([x], [x])
+    for _ in range(ways // 2):
+        earlier.append(lax.ppermute(earlier[-1], axis, up))
+    for _ in range((ways - 1) // 2):
+        later.append(lax.ppermute(later[-1], axis, down))
+    line = jnp.concatenate([*earlier[::-1], *later[1:]], axis=dim)
+    return jnp.roll(line, (lax.axis_index(axis) - ways // 2) * x.shape[dim], axis=dim)
 
 
 def scaled_norm(values, gain):
@@ -99,7 +112,7 @@
         lax.all_gather(first_gain, "fsdp", axis=0, tiled=True),
         lax.all_gather(first_shift, "fsdp", axis=0, tiled=True),
         lax.all_gather(joint_weight, "fsdp", axis=0, tiled=True),
-        lax.all_gather(joint_bias, "fsdp", axis=1, tiled=True),
+        collect(joint_bias, "fsdp", 1),
         lax.all_gather(output_weight, "fsdp", axis=0, tiled=True),
         lax.all_gather(output_bias, "fsdp", axis=0, tiled=True),
     )

time: 1130 us -> 1150 us (1.018)
  starting transfers between devices: 14.4 us -> 46.6 us
  blocking collectives: 218 us -> 194 us
  waiting for transfers between devices: 512 us -> 527 us
    ppermute x0 -> x15, starting transfers between devices: none -> 32.2 us  [the longest x7 31.6 us: collect(): later.append(lax.ppermute(later[-1], axis, down))]
    all_gather x1 -> x0, blocking collectives: 23.6 us -> none  [per_device(): lax.all_gather(joint_bias, 'fsdp', axis=1, tiled=True)]
    ppermute x0 -> x15, waiting for transfers between devices: none -> 13.3 us  [the longest x8 12.9 us: collect(): earlier.append(lax.ppermute(earlier[-1], axis, up))]
  transfers between devices with their start and end apart: 13 -> 28, of which waited for: 6 -> 17; matrix products, arithmetic and copies ran while one was open for 29% -> 28% of each run, Pallas kernels for 0% -> 0%
where the time goes in v1:
time: 1150 us; the launch traced here: 1140 us
  waiting for transfers between devices  527 us (46%)
  matrix products  226 us (20%)
  blocking collectives  194 us (17%)
  local copies, waits for them, and re-layouts  82.7 us (7%)
  other arithmetic  49.7 us (4%)
  starting transfers between devices  46.6 us (4%)
  between operations  17 us (1%)
    reduce_scatter x1, waiting for transfers between devices, per_device(): lax.psum_scatter(grad_up_weight, 'fsdp', scatter_dimension=0, tiled=True)  179 us
    reduce_scatter x1, waiting for transfers between devices, per_device(): lax.psum_scatter(grad_down_weight, 'fsdp', scatter_dimension=0, tiled=True)  179 us
    unnamed x2, blocking collectives  120 us
    dot_general x28, matrix products, right_contract(): lax.dot_general(left, right, (((1,), (1,)), ((), ())), preferred_element_...  100 us
    reduce_scatter x1, waiting for transfers between devices, per_device(): lax.psum_scatter(grad_joint_weight, 'fsdp', scatter_dimension=0, tiled=True)  80.7 us
    dot_general x20, matrix products, left_contract(): lax.dot_general(left, right, (((0,), (0,)), ((), ())), preferred_element_...  67.2 us
    dot_general x20, matrix products, matmul(): return jnp.dot(left, right, preferred_element_type=jnp.float32)  58.3 us
    all_to_all x1, blocking collectives, per_device(): lax.all_to_all(grad_stack, 'seq', split_axis=0, concat_axis=2, tiled=True)  51.4 us
  transfers between devices with their start and end apart: 28, of which 17 were waited for; matrix products, arithmetic and copies ran while one was open for 28% of the time, Pallas kernels for 0%

profile of v1, /device:TPU:0, one launch (start us, length us, event | category | flops | bytes accessed | tf_op | source)
XLA Modules:
  0.0 1143.6 jit_solution(2436061645783193778)
XLA Ops:
  10.1 5.0 collective-permute-start.8
  19.7 60.9 %all-reduce.14 = (bf16[1024]{0:T(1024)(128)(2,1)S(1)}, bf16[1024]{0:T(1024)(128)(2,1)S(1)}, bf16[1024]{0:T(1024)(128)(2,1)S(1)}, bf16[1024]{0:T(1024)(128)(2,1)}...) all-reduce(bf16[1024]{0:T(1024)(128)(2,1)S(1)} %dynamic-update-slic, ...), channel_id=1, replica_groups=mesh['seq'=2,'fsdp'=16] {'fsdp'}, use_global_device_ids=true, to_apply=%add.1 | all-reduce | flops 6144 | bytes 24576
  80.6 4.4 collective-permute-start.9
  103.5 4.5 collective-permute-start.13
  115.0 5.6 collective-permute-done.7
  120.8 7.9 add_convert_fusion
  128.8 8.3 reshape.247
  137.0 8.7 copy.69
  145.7 5.7 all-to-all-start
  151.4 32.0 %all-to-all-done = bf16[512,3,2,512]{0,3,1,2:T(8,128)(2,1)} async-done(((bf16[512,3,2,512]{0,3,1,2:T(8,128)(2,1)}), bf16[512,3,2,512]{0,3,1,2:T(8,128)(2,1)}, u32[]{:S(2)}, u32[]{:S(2)}) %all-to-all-start) | async-done | bytes 3145760 | tf_op jit(solution)/shard_map/all_to_all | solution.py:127
  183.4 6.8 copy.70
  190.2 6.2 reshape.248
  205.3 47.9 %while.24 = (s32[]{:T(128)}, bf16[8,1024,64]{1,2,0:T(8,128)(2,1)}, f32[8,1024]{1,0:T(8,128)S(1)}, bf16[8,1024,64]{2,1,0:T(8,128)(2,1)}, bf16[8,1024,64]{2,1,0:T(...) while((s32[]{:T(128)}, bf16[8,1024,64]{1,2,0:T(8,128)(2,1)}, ...), condition=%wide.region_5.6_spmd.clone, body=%wide.region_2.5_spmd.clone.sunk | while | flops 282131456 | bytes 13548157 | solution.py:66
  266.5 17.3 %all-gather = bf16[16,1,256]{2,1,0:T(2,128)(2,1)S(1)} all-gather(bf16[1,1,256]{2,1,0:T(2,128)(2,1)S(1)} %reshape.273), channel_id=1, replica_groups=mesh['seq'=2,'fsdp'=16] {'fsdp'}, dimensions={0}, use_global_device_ids=true | all-gather | bytes 8704 | tf_op jit(solution)/shard_map/all_gather | solution.py:145
  293.0 10.7 fusion.109
  303.7 14.0 %convert_reduce_fusion = (f32[4096]{0:T(1024)}, bf16[512,4096]{1,0:T(8,128)(2,1)S(1)}) fusion(f32[512,4096]{1,0:T(8,128)} %fusion.109, f32[4096]{0:T(1024)S(1)} %bitcast.233, bf16[4096,1024]{1,0:T(8,128)(2,1)} %all-gather.12.cloned.1.call-done, bf16[1,512,1024]{2,1,0:T(8,128)(2,1)S(1)} %copy-done.6), kind=kOutput, calls=%fused_computation.72 | convolution fusion | flops 4343197696 | bytes 22052864 | tf_op jit(solution)/shard_map/dot_general | solution.py:45
  317.7 5.0 multiply_reduce_fusion.1
  335.5 11.1 all-to-all-done.2
  348.9 99.7 %while.25 = (s32[]{:T(128)}, bf16[8,3,1024,64]{2,3,0,1:T(8,128)(2,1)}, bf16[8,1024,64]{2,1,0:T(8,128)(2,1)}, bf16[8,1024,64]{2,1,0:T(8,128)(2,1)}, f32[8]{0:T(12...) while((s32[]{:T(128)}, ...), condition=%wide.region_12.13_spmd.clone, body=%wide.region_10.12_spmd.clone.sunk | while | flops 688323584 | bytes 34241164 | solution.py:84
  448.6 7.6 copy.83
  456.2 51.4 %all_to_all.60 = bf16[1024,3,1,512]{3,1,2,0:T(4,128)(2,1)S(1)} all-to-all(bf16[1024,3,1,512]{3,1,2,0:T(4,128)(2,1)} %copy.83), channel_id=1, replica_groups=mesh['seq'=2,'fsdp'=16] {'seq'}, dimensions={0} | all-to-all | bytes 6291456 | tf_op jit(solution)/shard_map/all_to_all | solution.py:188
  511.3 10.5 fusion.88
  522.0 15.7 %fusion.108 = f32[1024,4096]{1,0:T(8,128)} fusion(bf16[512,4096]{1,0:T(8,128)(2,1)} %copy-done.34, f32[512,1024]{1,0:T(8,128)} %copy-done.4, f32[1024]{0:T(1024)S(1)} %convert_element_type.192, f32[1024]{0:T(1024)S(1)} %convert_element_type.191, f32[512]{0:T(512)S(1)} %fusion.106, f32[512]{0:T(512)S(1)} %broadcast_multiply_fusion), kind=kOutput, calls=%fused_computation.153 | convolution fusion | flops 4297588736 | bytes 23080960 | tf_op jit(solution)/shard_map/dot_general | solution.py:39
  537.8 17.8 %fusion.91 = f32[4096,1024]{1,0:T(8,128)} fusion(bf16[1,512,1024]{2,1,0:T(8,128)(2,1)} %param.33, f32[512,4096]{1,0:T(8,128)} %fusion.109, f32[4096]{0:T(1024)S(1)} %bitcast.234), kind=kOutput, calls=%fused_computation.116 | convolution fusion | flops 4315938816 | bytes 26230784 | tf_op jit(solution)/shard_map/dot_general | solution.py:39
  559.4 12.9 %fusion.85 = bf16[1,512,1024]{2,1,0:T(8,128)(2,1)} fusion(f32[512,1024]{1,0:T(8,128)} %copy-done.4, bf16[4096,1024]{1,0:T(8,128)(2,1)} %all-gather.12.cloned.1.call-done, f32[1024]{0:T(1024)S(1)} %convert_element_type.196, f32[512,4096]{1,0:T(8,128)} %fusion.109, f32[4096]{0:T(1024)S(1)} %bitcast.235), kind=kOutput, calls=%fused_computation.109 | convolution fusion | flops 4317511680 | bytes 19943424 | tf_op jit(solution)/shard_map/dot_general | solution.py:35
  574.0 80.7 %reduce-scatter.8.cloned.1.call-done = f32[64,3072]{1,0:T(8,128)} async-done(((f32[1024,3072]{1,0:T(8,128)}), f32[64,3072]{1,0:T(8,128)}) %reduce-scatter.8.cloned.1.call-update) | async-done | bytes 786448 | tf_op jit(solution)/shard_map/reduce_scatter | solution.py:201
  656.7 178.8 %reduce-scatter.12.cloned.1.call-done = f32[64,4096]{1,0:T(8,128)} async-done(((f32[1024,4096]{1,0:T(8,128)}), f32[64,4096]{1,0:T(8,128)}) %reduce-scatter.12.cloned.1.call-update) | async-done | bytes 1048592 | tf_op jit(solution)/shard_map/reduce_scatter | solution.py:207
  837.5 178.5 %reduce-scatter.14.cloned.1.call-done = f32[256,1024]{1,0:T(8,128)} async-done(((f32[4096,1024]{1,0:T(8,128)}), f32[256,1024]{1,0:T(8,128)}) %reduce-scatter.14.cloned.1.call-update) | async-done | bytes 1048592 | tf_op jit(solution)/shard_map/reduce_scatter | solution.py:209
  1018.2 6.9 fusion.110
  1029.1 59.6 %all-reduce.13 = (bf16[1024]{0:T(1024)(128)(2,1)S(1)}, bf16[1024]{0:T(1024)(128)(2,1)S(1)}, bf16[1024]{0:T(1024)(128)(2,1)S(1)}, bf16[1024]{0:T(1024)(128)(2,1)S...) all-reduce(f32[1024]{0:T(1024)S(1)} %get-tuple-element.229, ...), channel_id=2, replica_groups=mesh['seq'=2,'fsdp'=16] {'fsdp'}, use_global_device_ids=true, to_apply=%region_16.17.clone | all-reduce | flops 10240 | bytes 61440
  1090.1 5.1 all-reduce.15
  1099.4 30.4 %all-reduce.19.cloned.1.call-done = (bf16[64,3072]{1,0:T(8,128)(2,1)}, bf16[64,1024]{1,0:T(8,128)(2,1)}, bf16[64,4096]{1,0:T(8,128)(2,1)}, bf16[256,1024]{1,0:T(8,128)(2,1)}) async-done(((bf16[64,3072]{1,0:T(8,128)(2,1)}, bf16[64,1024]{1,0:T(8,128)(2,1)}, bf16[64,4096]{1,0:T(8,128)(2,1)}, bf16[256,1024]{1,0:T(8,128)(2,1)}), (bf16[64,3072]{1,0:T(8,128)(2,1)}, bf16[64,1024]{1,0:T(8,128)(2,1)}, ...) | async-done | bytes 1572880 | tf_op jit(solution)/shard_map/psum | solution.py:217
  (338 shorter events, 256.1 us)
Async XLA Ops:
  7.2 113.4 %copy-start.23 = (bf16[2,64]{1,0:T(2,128)(2,1)S(1)}, bf16[2,64]{1,0:T(2,128)(2,1)}, u32[]{:S(2)}) copy-start(bf16[2,64]{1,0:T(2,128)(2,1)} %param.24) | copy-start | bytes 772
  7.3 113.6 %all-gather.6.cloned.1.call-start = ((), (), s32[]{:S(2)}) async-start(), calls=%async_computation.9 | async-start | bytes 6684672 | tf_op jit(solution)/shard_map/all_gather | solution.py:114
  8.0 281.3 %all-gather.8.cloned.1.call-start = ((), (), s32[]{:S(2)}) async-start(), calls=%async_computation.10 | async-start | bytes 2228224 | tf_op jit(solution)/shard_map/all_gather | solution.py:116
  8.8 284.3 %all-gather.10.cloned.1.call-start = ((), (), s32[]{:S(2)}) async-start(), calls=%async_computation.11 | async-start | bytes 8912896 | tf_op jit(solution)/shard_map/all_gather | solution.py:144
  9.5 294.2 %all-gather.12.cloned.1.call-start = ((), (), s32[]{:S(2)}) async-start(), calls=%async_computation.12 | async-start | bytes 8912896 | tf_op jit(solution)/shard_map/all_gather | solution.py:146
  9.5 71.1 %collective-permute-start = (bf16[2,64]{1,0:T(2,128)(2,1)}, bf16[2,64]{1,0:T(2,128)(2,1)S(1)}, u32[]{:S(2)}, u32[]{:S(2)}) collective-permute-start(bf16[2,64]{1,0:T(2,128)(2,1)} %param.24), channel_id=1, source_target_pairs={{0,1},{1,2},{2,3},{3,4},{4,5},{5,6},{6,7},{7,8},{8,9},{9,10},{10,1... | collective-permute-start | bytes 776 | tf_op jit(solution)/shard_map/ppermute | solution.py:17
  10.1 70.5 %collective-permute-start.8 = (bf16[2,64]{1,0:T(2,128)(2,1)}, bf16[2,64]{1,0:T(2,128)(2,1)S(1)}, u32[]{:S(2)}, u32[]{:S(2)}) collective-permute-start(bf16[2,64]{1,0:T(2,128)(2,1)} %param.24), channel_id=1, source_target_pairs={{0,15},{1,0},{2,1},{3,2},{4,3},{5,4},{6,5},{7,6},{8,7},{9,8},{10,9... | collective-permute-start | bytes 776 | tf_op jit(solution)/shard_map/ppermute | solution.py:19
  16.6 112.2 %copy-start.13 = (f32[512]{0:T(512)}, f32[512]{0:T(512)S(1)}, u32[]{:S(2)}) copy-start(f32[512]{0:T(512)S(1)} %broadcast_multiply_fusion.1) | copy-start | bytes 6148
  17.0 111.7 %copy-start.15 = (f32[512]{0:T(512)}, f32[512]{0:T(512)S(1)}, u32[]{:S(2)}) copy-start(f32[512]{0:T(512)S(1)} %fusion.105) | copy-start | bytes 6148
  80.6 5.7 collective-permute-start.1
  80.6 5.7 collective-permute-start.9
  86.3 5.7 collective-permute-start.2
  86.4 5.7 collective-permute-start.10
  92.0 5.7 collective-permute-start.3
  92.1 5.7 collective-permute-start.11
  97.7 5.7 collective-permute-start.4
  97.8 5.7 collective-permute-start.12
  103.4 5.8 collective-permute-start.5
  103.5 5.8 collective-permute-start.13
  109.2 5.7 collective-permute-start.6
  109.3 5.7 collective-permute-start.14
  114.9 5.7 collective-permute-start.7
  145.7 37.7 %all-to-all-start = ((bf16[512,3,2,512]{0,3,1,2:T(8,128)(2,1)}), bf16[512,3,2,512]{0,3,1,2:T(8,128)(2,1)}, u32[]{:S(2)}, u32[]{:S(2)}) async-start(bf16[512,3,2,512]{0,3,1,2:T(8,128)(2,1)} %copy.69), calls=%async_computation | async-start | bytes 6291456 | tf_op jit(solution)/shard_map/all_to_all | solution.py:127
  262.0 21.8 %all-to-all-start.1 = ((bf16[2,2,131072]{2,1,0:T(2,128)(2,1)}), bf16[2,2,131072]{2,1,0:T(2,128)(2,1)}, u32[]{:S(2)}, u32[]{:S(2)}) async-start(bf16[2,2,131072]{2,1,0:T(2,128)(2,1)} %reshape.299), calls=%async_computation.1 | async-start | bytes 2097152 | tf_op jit(solution)/shard_map/all_to_all | solution.py:137
  328.4 18.2 %all-to-all-start.2 = ((bf16[512,2,512]{0,2,1:T(8,128)(2,1)}), bf16[512,2,512]{0,2,1:T(8,128)(2,1)S(1)}, u32[]{:S(2)}, u32[]{:S(2)}) async-start(bf16[512,2,512]{0,2,1:T(8,128)(2,1)} %bitcast.16), calls=%async_computation.2 | async-start | bytes 2097152 | tf_op jit(solution)/shard_map/all_to_all | solution.py:184
  332.0 240.3 %reduce-scatter.10.cloned.1.call-start = ((), (), s32[]{:S(2)}) async-start(), calls=%async_computation.14 | async-start | bytes 4456448 | tf_op jit(solution)/shard_map/reduce_scatter | solution.py:203
  335.4 319.3 %reduce-scatter.8.cloned.1.call-start = ((), (), s32[]{:S(2)}) async-start(), calls=%async_computation.13 | async-start | bytes 13369344 | tf_op jit(solution)/shard_map/reduce_scatter | solution.py:201
  521.8 313.7 %reduce-scatter.12.cloned.1.call-start = ((), (), s32[]{:S(2)}) async-start(), calls=%async_computation.15 | async-start | bytes 17825792 | tf_op jit(solution)/shard_map/reduce_scatter | solution.py:207
  537.8 478.3 %reduce-scatter.14.cloned.1.call-start = ((), (), s32[]{:S(2)}) async-start(), calls=%async_computation.16 | async-start | bytes 17825792 | tf_op jit(solution)/shard_map/reduce_scatter | solution.py:209
  555.7 533.6 %reduce-scatter.16.cloned.1.call-start = ((), (), s32[]{:S(2)}) async-start(), calls=%async_computation.17 | async-start | bytes 557056
  559.2 570.6 %all-reduce.19.cloned.1.call-start = ((), (), s32[]{:S(2)}) async-start(), calls=%async_computation.18 | async-start | bytes 3145728 | tf_op jit(solution)/shard_map/psum | solution.py:217
  572.3 445.9 %copy-start.1 = (bf16[1,512,1024]{2,1,0:T(8,128)(2,1)S(1)}, bf16[1,512,1024]{2,1,0:T(8,128)(2,1)}, u32[]{:S(2)}) copy-start(bf16[1,512,1024]{2,1,0:T(8,128)(2,1)} %param.19) | copy-start | bytes 3145732
  (31 other events, 335.9 us)
Sparse Core Ops, SparseCore 0:
  10.4 64.6 all-gather.5
  77.3 40.1 all-gather.7
  119.7 73.0 all-gather.9
  194.8 72.9 all-gather.11
  336.4 71.8 reduce-scatter.9
  521.9 132.7 reduce-scatter.7
  658.9 176.5 reduce-scatter.11
  839.6 176.4 reduce-scatter.13
  1020.2 55.3 reduce-scatter.15
  1079.0 50.6 all-reduce.18
